TPU v7x, 256 devices: a whole 4x4x8 slice. The times are simulated.
256 devices in a mesh: dom: 16 (over z, x_lo), ref: 16 (over x_hi, y, core).
Axes of the slice: x: 4 (x_hi: 2, x_lo: 2; x = x_hi * 2 + x_lo), y: 4, z: 8, core: 2. Of those that a mesh axis runs over, the one named last changes fastest.
Arguments:
- particles: float32 [8192, 128], P('dom'), may hold values from -1.2 to 1.2
- references: float32 [16384, 128], P('ref'), may hold values from -1 to 1.2
Outputs:
- moved: float32 [8192, 128], P(('dom', 'ref'))
- drift: float32 [8192, 128], P(('dom', 'ref'))
All inputs are finite; a program needn't handle non-finite values.
Results may differ from a plain program's by a relative error of at most 0.00035.
Values sent between devices are 32-bit elements; how exact they have to be, the bound alone decides.
A program may use at most 64 MiB of HBM per device.

v0:
```python
import jax
import jax.numpy as jnp
from jax import lax
from jax.sharding import PartitionSpec as P

STEPS = 2
step_size = 0.5


def kernel_terms(block, others):
    inner = jnp.dot(
        block, others.T, precision=lax.Precision.HIGHEST, preferred_element_type=jnp.float32
    )
    squared = (
        jnp.sum(block * block, axis=1)[:, None]
        + jnp.sum(others * others, axis=1)[None, :]
        - 2.0 * inner
    )
    weights = jnp.exp(-0.5 * squared)
    pulled = jnp.dot(
        weights, others, precision=lax.Precision.HIGHEST, preferred_element_type=jnp.float32
    )
    return (pulled, jnp.sum(weights, axis=1))


def partial_gradient(block, own_rows, references, count_p, count_r):
    pulled, summed = kernel_terms(block, lax.all_gather(own_rows, "dom", axis=0, tiled=True))
    pull_r, sum_r = kernel_terms(block, references)
    return (pulled - summed[:, None] * block) / count_p - (
        pull_r - sum_r[:, None] * block
    ) / count_r


def on_device(particles, references):
    n_ref = lax.axis_size("ref")
    n_dom = lax.axis_size("dom")
    rows = particles.shape[0] // n_ref
    count_p = particles.shape[0] * n_dom
    count_r = references.shape[0] * n_ref
    offset = lax.axis_index("ref") * rows
    start_rows = lax.dynamic_slice_in_dim(particles, offset, rows, 0)
    block = particles
    own_rows = start_rows
    for step in range(STEPS):
        partial_value = partial_gradient(block, own_rows, references, count_p, count_r)
        gradient = lax.psum(partial_value, "ref")
        block = block - step_size * gradient
        own_rows = lax.dynamic_slice_in_dim(block, offset, rows, 0)
    return (own_rows, (own_rows - start_rows) / step_size)


def solution(mesh):
    placed = (P("dom", None), P("ref", None))
    return jax.shard_map(
        on_device,
        mesh=mesh,
        in_specs=placed,
        out_specs=(P(("dom", "ref"), None), P(("dom", "ref"), None)),
        check_vma=False,
    )
```

profile of v0, /device:TPU:1, one launch (start us, length us, event | category | flops | bytes accessed | tf_op | source)
XLA Modules:
  0.0 391.9 jit_solution(12961687768505106673)
XLA Ops:
  7.2 0.0 copy-start
  7.2 0.0 copy-start.1
  7.2 0.0 all-reduce.3.cloned.1.call-start
  7.2 1.2 multiply_reduce_fusion.4
  8.4 1.2 multiply_reduce_fusion
  9.7 0.7 constant_dynamic-slice_fusion.1
  10.4 31.7 %all_gather.6 = f32[512,128]{1,0:T(8,128)S(1)} all-gather(f32[32,128]{1,0:T(8,128)S(1)} %constant_dynamic-slice_fusion.1), channel_id=1, replica_groups=mesh['dom'=16,'ref'=16] {'dom'}, dimensions={0}, use_global_device_ids=true | all-gather | bytes 278528 | tf_op jit(solution)/shard_map/all_gather | solution.py:27
  42.1 0.1 multiply_reduce_fusion.3
  42.2 2.1 fusion.15
  44.3 0.0 copy-done
  44.4 0.0 copy-done.1
  44.4 2.3 fusion.16
  46.7 1.8 fusion.12
  48.5 2.5 fusion.9
  51.0 0.0 all-reduce.3.cloned.1.call-update
  51.1 0.0 all-reduce.5.cloned.1.call-start
  51.1 148.4 %all-reduce.3.cloned.1.call-done = f32[512,128]{1,0:T(8,128)} async-done(((f32[512,128]{1,0:T(8,128)}), f32[512,128]{1,0:T(8,128)}) %all-reduce.3.cloned.1.call-update) | async-done | bytes 262160 | tf_op jit(solution)/shard_map/psum | solution.py:46
  199.5 1.1 multiply_reduce_fusion.2
  200.7 27.7 %all_gather.7 = f32[512,128]{1,0:T(8,128)S(1)} all-gather(f32[32,128]{1,0:T(8,128)S(1)} %constant_dynamic-slice_fusion), channel_id=1, replica_groups=mesh['dom'=16,'ref'=16] {'dom'}, dimensions={0}, use_global_device_ids=true | all-gather | bytes 278528 | tf_op jit(solution)/shard_map/all_gather | solution.py:27
  228.4 0.1 multiply_reduce_fusion.1
  228.5 2.3 fusion.18
  230.8 1.2 fusion.17
  232.1 1.8 fusion.11
  233.9 2.5 fusion.10
  236.4 0.0 all-reduce.5.cloned.1.call-update
  236.5 147.3 %all-reduce.5.cloned.1.call-done = f32[512,128]{1,0:T(8,128)} async-done(((f32[512,128]{1,0:T(8,128)}), f32[512,128]{1,0:T(8,128)}) %all-reduce.5.cloned.1.call-update) | async-done | bytes 262160 | tf_op jit(solution)/shard_map/psum | solution.py:46
  383.7 1.3 subtract_multiply_fusion
  (1 shorter events, 0.0 us)
Async XLA Ops:
  7.2 37.2 %copy-start = (f32[512,128]{1,0:T(8,128)S(1)}, f32[512,128]{1,0:T(8,128)}, u32[]{:S(2)}) copy-start(f32[512,128]{1,0:T(8,128)} %param.2) | copy-start | bytes 786436
  7.2 37.2 %copy-start.1 = (f32[1024,128]{1,0:T(8,128)S(1)}, f32[1024,128]{1,0:T(8,128)}, u32[]{:S(2)}) copy-start(f32[1024,128]{1,0:T(8,128)} %param.3) | copy-start | bytes 1572868
  7.2 192.4 %all-reduce.3.cloned.1.call-start = ((), (), s32[]{:S(2)}) async-start(), calls=%async_computation | async-start | bytes 524288 | tf_op jit(solution)/shard_map/psum | solution.py:46
  51.1 332.7 %all-reduce.5.cloned.1.call-start = ((), (), s32[]{:S(2)}) async-start(), calls=%async_computation.1 | async-start | bytes 524288 | tf_op jit(solution)/shard_map/psum | solution.py:46
Sparse Core Ops, SparseCore 0:
  51.2 148.3 all-reduce.2
  236.6 147.0 all-reduce.4
where the time goes:
time: 392 us
  waiting for transfers between devices  296 us (76%)
  blocking collectives  59.4 us (15%)
  matrix products  16.7 us (4%)
  between operations  14.1 us (4%)
  other arithmetic  5.12 us (1%)
    psum x2, waiting for transfers between devices, on_device(): gradient = lax.psum(partial_value, 'ref')  296 us
    all_gather x2, blocking collectives, partial_gradient(): lax.all_gather(own_rows, 'dom', axis=0, tiled=True)  59.4 us
    dot_general x4, matrix products, kernel_terms(): jnp.dot(weights, others, precision=lax.Precision.HIGHEST, preferred_eleme...  8.73 us
    dot_general x4, matrix products, kernel_terms(): jnp.dot(block, others.T, precision=lax.Precision.HIGHEST, preferred_eleme...  7.95 us
  transfers between devices with their start and end apart: 2, of which 2 were waited for; matrix products, arithmetic and copies ran while one was open for 0% of the time, Pallas kernels for 0%

commit v1 on v0

--- a/solution.py
+++ b/solution.py
@@ -5,6 +5,11 @@
 
 STEPS = 2
 step_size = 0.5
+
+
+def add_all(array, name):
+    parts = lax.all_gather(array, name)
+    return jnp.sum(parts, axis=0)
 
 
 def kernel_terms(block, others):
@@ -43,7 +48,7 @@
     own_rows = start_rows
     for step in range(STEPS):
         partial_value = partial_gradient(block, own_rows, references, count_p, count_r)
-        gradient = lax.psum(partial_value, "ref")
+        gradient = add_all(partial_value, "ref")
         block = block - step_size * gradient
         own_rows = lax.dynamic_slice_in_dim(block, offset, rows, 0)
     return (own_rows, (own_rows - start_rows) / step_size)

time: 392 us -> 227 us (0.58)
  waiting for transfers between devices: 296 us -> 128 us
    psum x2 -> x0, waiting for transfers between devices: 296 us -> none  [on_device(): gradient = lax.psum(partial_value, 'ref')]
    all_gather x0 -> x2, waiting for transfers between devices: none -> 128 us  [add_all(): parts = lax.all_gather(array, name)]
    reduce_sum x0 -> x2, other arithmetic: none -> 4.81 us  [add_all(): return jnp.sum(parts, axis=0)]
where the time goes in v1:
time: 227 us; the launch traced here: 226 us
  waiting for transfers between devices  128 us (56%)
  blocking collectives  58.9 us (26%)
  matrix products  16.5 us (7%)
  between operations  14.1 us (6%)
  other arithmetic  8.28 us (4%)
    all_gather x2, waiting for transfers between devices, add_all(): parts = lax.all_gather(array, name)  128 us
    all_gather x2, blocking collectives, partial_gradient(): lax.all_gather(own_rows, 'dom', axis=0, tiled=True)  58.9 us
    dot_general x4, matrix products, kernel_terms(): jnp.dot(weights, others, precision=lax.Precision.HIGHEST, preferred_eleme...  8.59 us
    dot_general x4, matrix products, kernel_terms(): jnp.dot(block, others.T, precision=lax.Precision.HIGHEST, preferred_eleme...  7.88 us
    reduce_sum x2, other arithmetic, add_all(): return jnp.sum(parts, axis=0)  4.81 us
  transfers between devices with their start and end apart: 2, of which 2 were waited for; matrix products, arithmetic and copies ran while one was open for 0% of the time, Pallas kernels for 0%

profile of v1, /device:TPU:1, one launch (start us, length us, event | category | flops | bytes accessed | tf_op | source)
XLA Modules:
  0.0 226.5 jit_solution(16002464640386293017)
XLA Ops:
  7.2 0.0 copy-start
  7.2 0.0 copy-start.1
  7.2 0.0 all-gather.5.cloned.1.call-start
  7.2 1.2 multiply_reduce_fusion.4
  8.4 1.2 multiply_reduce_fusion
  9.7 0.7 constant_dynamic-slice_fusion.1
  10.4 31.7 %all_gather.18 = f32[512,128]{1,0:T(8,128)S(1)} all-gather(f32[32,128]{1,0:T(8,128)S(1)} %constant_dynamic-slice_fusion.1), channel_id=1, replica_groups=mesh['dom'=16,'ref'=16] {'dom'}, dimensions={0}, use_global_device_ids=true | all-gather | bytes 278528 | tf_op jit(solution)/shard_map/all_gather | solution.py:32
  42.1 0.1 multiply_reduce_fusion.3
  42.2 2.1 fusion.15
  44.3 0.0 copy-done
  44.4 0.0 copy-done.1
  44.4 2.3 %fusion.16 = (f32[512]{0:T(512)S(1)}, f32[512,1024]{1,0:T(8,128)S(1)}) fusion(f32[512,128]{1,0:T(8,128)S(1)} %copy-done, f32[1024,128]{1,0:T(8,128)S(1)} %copy-done.1, f32[1024]{0:T(1024)S(1)} %multiply_reduce_fusion, f32[512]{0:T(512)S(1)} %multiply_reduce_fusion.4), kind=kOutput, calls=%fused_computation.33 | convolution fusion | flops 807927296 | bytes 2891776 | tf_op jit(solution)/shard_map/dot_general | solution.py:16
  46.6 1.8 fusion.12
  48.5 2.5 %fusion.9 = f32[512,128]{1,0:T(8,128)} fusion(f32[512,128]{1,0:T(8,128)S(1)} %fusion.12, f32[512,1024]{1,0:T(8,128)S(1)} %get-tuple-element.9, f32[1024,128]{1,0:T(8,128)S(1)} %copy-done.1, f32[512,128]{1,0:T(8,128)S(1)} %copy-done, f32[512]{0:T(512)S(1)} %get-tuple-element.8), kind=kOutput, calls=%fused_computation.15 | convolution fusion | flops 805568512 | bytes 3409920 | tf_op jit(solution)/shard_map/dot_general | solution.py:25
  50.9 0.0 all-gather.5.cloned.1.call-update
  51.0 0.0 all-gather.7.cloned.1.call-start
  51.0 64.6 %all-gather.5.cloned.1.call-done = f32[8192,128]{1,0:T(8,128)} async-done(((f32[512,128]{1,0:T(8,128)}), f32[8192,128]{1,0:T(8,128)}) %all-gather.5.cloned.1.call-update) | async-done | bytes 4194320 | tf_op jit(solution)/shard_map/all_gather | solution.py:11
  115.6 2.4 %reduce_sum.116 = f32[512,128]{1,0:T(8,128)S(1)} reduce(f32[16,512,128]{2,1,0:T(8,128)} %bitcast.26, f32[]{:T(128)} %constant.10.clone.1), dimensions={0}, to_apply=%region_5.0 | reduce | flops 983040 | bytes 4456452 | tf_op jit(solution)/shard_map/reduce_sum | solution.py:12
  118.0 0.1 multiply_reduce_fusion.2
  118.2 27.3 %all_gather.21 = f32[512,128]{1,0:T(8,128)S(1)} all-gather(f32[32,128]{1,0:T(8,128)S(1)} %constant_dynamic-slice_fusion), channel_id=1, replica_groups=mesh['dom'=16,'ref'=16] {'dom'}, dimensions={0}, use_global_device_ids=true | all-gather | bytes 278528 | tf_op jit(solution)/shard_map/all_gather | solution.py:32
  145.5 0.1 multiply_reduce_fusion.1
  145.6 2.3 %fusion.18 = (f32[512]{0:T(512)S(1)}, f32[512,1024]{1,0:T(8,128)S(1)}) fusion(f32[512,128]{1,0:T(8,128)S(1)} %get-tuple-element.5, f32[1024,128]{1,0:T(8,128)S(1)} %copy-done.1, f32[1024]{0:T(1024)S(1)} %multiply_reduce_fusion, f32[512]{0:T(512)S(1)} %get-tuple-element.4), kind=kOutput, calls=%fused_computation.35 | convolution fusion | flops 807927296 | bytes 2891776 | tf_op jit(solution)/shard_map/dot_general | solution.py:16
  147.9 1.2 fusion.17
  149.1 1.8 fusion.11
  150.9 2.5 %fusion.10 = f32[512,128]{1,0:T(8,128)} fusion(f32[512,128]{1,0:T(8,128)S(1)} %fusion.11, f32[512,1024]{1,0:T(8,128)S(1)} %get-tuple-element.13, f32[1024,128]{1,0:T(8,128)S(1)} %copy-done.1, f32[512,128]{1,0:T(8,128)S(1)} %get-tuple-element.5, f32[512]{0:T(512)S(1)} %get-tuple-element.12), kind=kOutput, calls=%fused_computation.16 | convolution fusion | flops 805568512 | bytes 3409920 | tf_op jit(solution)/shard_map/dot_general | solution.py:25
  153.4 0.0 all-gather.7.cloned.1.call-update
  153.4 63.2 %all-gather.7.cloned.1.call-done = f32[8192,128]{1,0:T(8,128)} async-done(((f32[512,128]{1,0:T(8,128)}), f32[8192,128]{1,0:T(8,128)}) %all-gather.7.cloned.1.call-update) | async-done | bytes 4194320 | tf_op jit(solution)/shard_map/all_gather | solution.py:11
  216.6 2.4 %reduce_sum.121 = f32[512,128]{1,0:T(8,128)S(1)} reduce(f32[16,512,128]{2,1,0:T(8,128)} %bitcast.27, f32[]{:T(128)} %constant.10.clone.1), dimensions={0}, to_apply=%region_10.0 | reduce | flops 983040 | bytes 4456452 | tf_op jit(solution)/shard_map/reduce_sum | solution.py:12
  219.0 0.6 subtract_multiply_fusion
  (1 shorter events, 0.0 us)
Async XLA Ops:
  7.2 37.2 %copy-start = (f32[512,128]{1,0:T(8,128)S(1)}, f32[512,128]{1,0:T(8,128)}, u32[]{:S(2)}) copy-start(f32[512,128]{1,0:T(8,128)} %param.2) | copy-start | bytes 786436
  7.2 37.2 %copy-start.1 = (f32[1024,128]{1,0:T(8,128)S(1)}, f32[1024,128]{1,0:T(8,128)}, u32[]{:S(2)}) copy-start(f32[1024,128]{1,0:T(8,128)} %param.3) | copy-start | bytes 1572868
  7.2 108.4 %all-gather.5.cloned.1.call-start = ((), (), s32[]{:S(2)}) async-start(), calls=%async_computation | async-start | bytes 4456448 | tf_op jit(solution)/shard_map/all_gather | solution.py:11
  51.0 165.6 %all-gather.7.cloned.1.call-start = ((), (), s32[]{:S(2)}) async-start(), calls=%async_computation.1 | async-start | bytes 4456448 | tf_op jit(solution)/shard_map/all_gather | solution.py:11
Sparse Core Ops, SparseCore 0:
  51.1 64.4 all-gather.4
  153.5 63.0 all-gather.6
